TPU v7x, 512 devices: a whole 4x4x16 slice. The times are simulated.
512 devices in a mesh: wide: 64 (over z, x), narrow: 8 (over y, core).
Axes of the slice: x: 4, y: 4, z: 16, core: 2. Of those that a mesh axis runs over, the one named last changes fastest.
Arguments:
- integrals: bfloat16 [16384, 65536], P('wide', 'narrow'), may hold values from -0.0625 to 0.0625
- amp_tiles: bfloat16 [8, 786432], P('narrow', 'wide'), may hold values from -6 to 6
- row_orbitals: int32 [16384, 2], P('wide'), may hold values from 0 to 511
- orb_irrep: int32 [512], replicated, may hold values from 0 to 3
- occ_pairs: int32 [96, 2], replicated, may hold values from 0 to 15
- occ_irrep: int32 [16], replicated, may hold values from 0 to 3
Outputs:
- residual: float32 [16384, 96], P(('wide', 'narrow'))
All inputs are finite; a program needn't handle non-finite values.
Results may differ from a plain program's by a relative error of at most 0.0003.
Values may be sent and summed in bfloat16 or wider, within the bound.
A program may use at most 64 MiB of HBM per device.

v0:
```python
import jax
import jax.numpy as jnp
from jax import lax
from jax.sharding import PartitionSpec as P


def lookup_irrep(orbitals, table):
    hits = orbitals[..., None] == jnp.arange(table.shape[0], dtype=jnp.int32)
    return jnp.sum(jnp.where(hits, table, 0), axis=-1)


def shards(integrals, amp_tiles, row_orbitals, orb_irrep, occ_pairs, occ_irrep):
    pair_count = occ_pairs.shape[0]
    column_count = integrals.shape[1]
    row_labels = lookup_irrep(row_orbitals, orb_irrep)
    pair_labels = lookup_irrep(occ_pairs, occ_irrep)
    row_sym = jnp.bitwise_xor(row_labels[:, 0], row_labels[:, 1])
    pair_sym = jnp.bitwise_xor(pair_labels[:, 0], pair_labels[:, 1])
    keep = row_sym[:, None] == pair_sym[None, :]
    gathered = lax.all_gather(amp_tiles, "wide", axis=1, tiled=True)
    amplitudes = gathered.reshape(column_count, pair_count)
    block = jnp.dot(integrals, amplitudes, preferred_element_type=jnp.float32)
    return lax.psum_scatter(
        jnp.where(keep, block, jnp.zeros_like(block)), "narrow", scatter_dimension=0, tiled=True
    )


def solution(mesh):
    in_specs = (P("wide", "narrow"), P("narrow", "wide"), P("wide", None), P(), P(), P())
    out_specs = P(("wide", "narrow"), None)
    return jax.shard_map(shards, mesh=mesh, in_specs=in_specs, out_specs=out_specs, check_vma=False)
```

profile of v0, /device:TPU:1, one launch (start us, length us, event | category | flops | bytes accessed | tf_op | source)
XLA Modules:
  0.0 239.6 jit_solution(9293615291129486285)
XLA Ops:
  6.5 0.0 all-gather.2.cloned.1.call-start
  6.5 0.7 all-gather.2.cloned.1.call-update
  7.3 0.0 reduce-scatter.2.cloned.1.call-start
  7.3 0.8 select_reduce_fusion.1
  8.1 1.0 select_reduce_fusion
  9.1 142.4 %all-gather.2.cloned.1.call-done = bf16[1,786432]{1,0:T(2,128)(2,1)} async-done(((bf16[1,12288]{1,0:T(2,128)(2,1)}), bf16[1,786432]{1,0:T(2,128)(2,1)}) %all-gather.2.cloned.1.call-update) | async-done | bytes 1572880 | tf_op jit(solution)/shard_map/all_gather | solution.py:20
  151.5 34.8 %reduce = bf16[786432]{0:T(1024)(128)(2,1)} reduce(bf16[1,786432]{1,0:T(2,128)(2,1)} %all-gather.2.cloned.1.call-done, bf16[]{:T(256)} %constant.5), dimensions={0}, to_apply=%all_gather.3.reduce_sub_computation | reduce | bytes 3145730 | tf_op jit(solution)/shard_map/all_gather | solution.py:20
  186.3 3.2 %reshape.15 = bf16[8192,96]{1,0:T(8,128)(2,1)S(1)} reshape(bf16[786432]{0:T(1024)(128)(2,1)} %reduce) | data formatting | bytes 3145728 | tf_op jit(solution)/shard_map/reshape | solution.py:21
  189.5 4.1 %convolution_select_fusion = f32[256,96]{1,0:T(8,128)} fusion(bf16[256,8192]{1,0:T(8,128)(2,1)} %param.6, bf16[8192,96]{1,0:T(8,128)(2,1)S(1)} %reshape.15, s32[96]{0:T(128)S(1)} %xor_bitcast_fusion, s32[256]{0:T(256)S(1)} %bitcast.5), kind=kOutput, calls=%fused_computation | convolution fusion | flops 402702336 | bytes 5866880 | tf_op jit(solution)/shard_map/dot_general | solution.py:22
  193.6 0.0 reduce-scatter.2.cloned.1.call-update
  193.6 39.1 %reduce-scatter.2.cloned.1.call-done = f32[32,96]{1,0:T(8,128)} async-done(((f32[256,96]{1,0:T(8,128)}), f32[32,96]{1,0:T(8,128)}) %reduce-scatter.2.cloned.1.call-update) | async-done | bytes 12304 | tf_op jit(solution)/shard_map/reduce_scatter | solution.py:23
  (2 shorter events, 0.0 us)
Async XLA Ops:
  6.5 144.9 %all-gather.2.cloned.1.call-start = ((), (), s32[]{:S(2)}) async-start(), calls=%async_computation.1 | async-start | bytes 3194880 | tf_op jit(solution)/shard_map/all_gather | solution.py:20
  7.3 225.5 %reduce-scatter.2.cloned.1.call-start = ((), (), s32[]{:S(2)}) async-start(), calls=%async_computation.2 | async-start | bytes 147456 | tf_op jit(solution)/shard_map/reduce_scatter | solution.py:23
Sparse Core Ops, SparseCore 0:
  10.3 141.1 all-gather.1
  193.7 38.9 reduce-scatter.1
where the time goes:
time: 241 us; the launch traced here: 240 us
  waiting for transfers between devices  182 us (76%)
  other arithmetic  36.5 us (15%)
  between operations  13.4 us (6%)
  matrix products  4.07 us (2%)
  local copies, waits for them, and re-layouts  3.24 us (1%)
    all_gather x1, waiting for transfers between devices, shards(): gathered = lax.all_gather(amp_tiles, 'wide', axis=1, tiled=True)  142 us
    reduce_scatter x1, waiting for transfers between devices, shards(): lax.psum_scatter(jnp.where(keep, block, jnp.zeros_like(block)), 'narrow',...  39.1 us
    all_gather x1, other arithmetic, shards(): gathered = lax.all_gather(amp_tiles, 'wide', axis=1, tiled=True)  34.8 us
  transfers between devices with their start and end apart: 2, of which 2 were waited for; matrix products, arithmetic and copies ran while one was open for 1% of the time, Pallas kernels for 0%

commit v1 on v0

v1 whole, which is shorter than its diff:
```python
import functools

import jax
import jax.numpy as jnp
from jax import lax
from jax.experimental import pallas as pl
from jax.experimental.pallas import tpu as pltpu
from jax.sharding import PartitionSpec as P

MESH = pl.DeviceIdType.MESH
NX = 4
LANES = 128


def pair_lookup(orbitals, table):
    count, entries = orbitals.shape[1], table.shape[1]
    column = jnp.sum(
        jnp.where(
            lax.broadcasted_iota(jnp.int32, (entries, entries), 0)
            == lax.broadcasted_iota(jnp.int32, (entries, entries), 1),
            jnp.broadcast_to(table, (entries, entries)),
            0,
        ),
        axis=1,
        keepdims=True,
    )
    place = lax.broadcasted_iota(jnp.int32, (entries, count), 0)
    labels = [
        jnp.sum(jnp.where(place == orbitals[i : i + 1, :], column, 0), axis=0, keepdims=True) for i in range(2)
    ]
    return labels[0] ^ labels[1]


def kernel(
    amp_ref, integrals_ref, row_sym_ref, pair_sym_ref, out_ref,
    rows, upright, gathered, block, acc, parts, load_sem, arrive, sent, part_sent, part_arrive,
):
    n_wide, n_narrow = lax.axis_size("wide"), lax.axis_size("narrow")
    nz = n_wide // NX
    half = nz // 2
    pairs = gathered.shape[1]
    own_rows = out_ref.shape[0]
    wide, narrow = lax.axis_index("wide"), lax.axis_index("narrow")
    z, x = wide // NX, wide % NX

    def at(dz, dx):
        return ((z + dz + nz) % nz) * NX + (x + dx + NX) % NX

    load = pltpu.make_async_copy(integrals_ref, block, load_sem)
    load.start()

    barrier = pltpu.get_barrier_semaphore()
    for other in (at(1, 0), at(-1, 0), at(0, 1), at(0, -1)):
        pl.semaphore_signal(barrier, inc=1, device_id={"wide": other}, device_id_type=MESH)
    for step in range(1, n_narrow):
        pl.semaphore_signal(
            barrier, inc=1, device_id={"narrow": (narrow + step) % n_narrow}, device_id_type=MESH
        )

    period = 4 * pairs
    groups = amp_ref.shape[1] // period
    for g in range(groups):
        rows[g : g + 1, :] = amp_ref[0:1, g * period : (g + 1) * period].astype(jnp.float32)
    upright[...] = jnp.zeros_like(upright)
    for j in range(4):
        upright[pl.ds(j, groups, stride=4), 0:pairs] = rows[:, j * pairs : (j + 1) * pairs]
    gathered[wide] = upright[...].T[:pairs, :].astype(jnp.bfloat16)
    acc[...] = jnp.zeros_like(acc)

    pl.semaphore_wait(barrier, 4 + n_narrow - 1)

    def send(source, dz, dx):
        pltpu.make_async_remote_copy(
            src_ref=gathered.at[source],
            dst_ref=gathered.at[source],
            send_sem=sent,
            recv_sem=arrive.at[source],
            device_id={"wide": at(dz, dx)},
            device_id_type=MESH,
        ).start()

    def wait(source):
        pltpu.make_async_remote_copy(
            src_ref=gathered.at[source],
            dst_ref=gathered.at[source],
            send_sem=sent,
            recv_sem=arrive.at[source],
            device_id={"wide": at(1, 0)},
            device_id_type=MESH,
        ).wait_recv()

    def multiply(dz):
        wait(at(dz, 1))
        wait(at(dz, -2))
        base = ((z + dz + nz) % nz) * NX
        columns = pl.ds(pl.multiple_of(base * LANES, NX * LANES), NX * LANES)
        amplitudes = jnp.concatenate([gathered[base + i] for i in range(NX)], axis=1)
        acc[:, 0:pairs] += lax.dot_general(
            block[:, columns], amplitudes, (((1,), (1,)), ((), ())), preferred_element_type=jnp.float32
        )

    send(wide, 0, 1)
    send(wide, 1, 0)
    send(wide, -1, 0)
    send(wide, 0, -1)
    beside = at(0, -1)
    wait(beside)
    send(beside, 1, 0)
    send(beside, -1, 0)
    send(beside, 0, 1)
    load.wait()

    def step(d, carry):
        for sign, dx, outer, last in ((-1, 0, -1, half), (1, -1, 1, half), (1, 0, -1, half - 1), (-1, -1, 1, half - 1)):
            source = at(sign * d, dx)
            wait(source)
            if last == half:
                send(source, -sign, 0)
            else:
                @pl.when(d < last)
                def _():
                    send(source, -sign, 0)
            send(source, 0, outer)
        multiply(-(d - 1))

        @pl.when(d > 1)
        def _():
            multiply(d - 1)

        return carry

    lax.fori_loop(1, half, step, 0)
    for sign, dx, outer in ((-1, 0, -1), (1, -1, 1)):
        source = at(sign * half, dx)
        wait(source)
        send(source, 0, outer)
    multiply(-(half - 1))
    multiply(half - 1)
    multiply(-half)

    def part(step):
        to = (narrow + step) % n_narrow
        return pltpu.make_async_remote_copy(
            src_ref=acc.at[pl.ds(pl.multiple_of(to * own_rows, own_rows), own_rows)],
            dst_ref=parts.at[n_narrow - step],
            send_sem=part_sent.at[step],
            recv_sem=part_arrive.at[n_narrow - step],
            device_id={"narrow": to},
            device_id_type=MESH,
        )

    copies = [part(step) for step in range(1, n_narrow)]
    for copy in copies:
        copy.start()
    total = acc[pl.ds(pl.multiple_of(narrow * own_rows, own_rows), own_rows), :]
    for step, copy in zip(range(1, n_narrow), copies):
        pltpu.make_async_remote_copy(
            src_ref=parts.at[step],
            dst_ref=parts.at[step],
            send_sem=part_sent.at[step],
            recv_sem=part_arrive.at[step],
            device_id={"narrow": (narrow + step) % n_narrow},
            device_id_type=MESH,
        ).wait_recv()
        total += parts[step]
    keep = row_sym_ref[...] == pair_sym_ref[...]
    out_ref[...] = jnp.where(keep, total[:, 0:pairs], 0.0)
    for copy in copies:
        copy.wait_send()
    pltpu.make_async_remote_copy(
        src_ref=gathered.at[pl.ds(0, n_wide - 1)],
        dst_ref=gathered.at[pl.ds(0, n_wide - 1)],
        send_sem=sent,
        recv_sem=arrive.at[0],
        device_id={"wide": at(1, 0)},
        device_id_type=MESH,
    ).wait_send()


def lookup_irrep(orbitals, table):
    hits = orbitals[..., None] == jnp.arange(table.shape[0], dtype=jnp.int32)
    return jnp.sum(jnp.where(hits, table, 0), axis=-1)


def shards(n_wide, n_narrow, integrals, amp_tiles, row_orbitals, orb_irrep, occ_pairs, occ_irrep):
    pairs = occ_pairs.shape[0]
    n_rows, n_columns = integrals.shape
    own_rows = n_rows // n_narrow
    mine = lax.dynamic_slice_in_dim(row_orbitals, lax.axis_index("narrow") * own_rows, own_rows, 0)
    row_labels = lookup_irrep(mine, orb_irrep)
    pair_labels = lookup_irrep(occ_pairs, occ_irrep)
    row_sym = (row_labels[:, 0] ^ row_labels[:, 1])[:, None]
    pair_sym = (pair_labels[:, 0] ^ pair_labels[:, 1])[None, :]
    vmem = pl.BlockSpec(memory_space=pltpu.VMEM)
    anywhere = pl.BlockSpec(memory_space=pl.ANY)
    return pl.pallas_call(
        kernel,
        out_shape=jax.ShapeDtypeStruct((own_rows, pairs), jnp.float32),
        in_specs=[vmem, anywhere, vmem, vmem],
        out_specs=vmem,
        scratch_shapes=[
            pltpu.VMEM((LANES // 4, 4 * pairs), jnp.float32),
            pltpu.VMEM((LANES, LANES), jnp.float32),
            pltpu.VMEM((n_wide, pairs, LANES), jnp.bfloat16),
            pltpu.VMEM((n_rows, n_columns), jnp.bfloat16),
            pltpu.VMEM((n_rows, LANES), jnp.float32),
            pltpu.VMEM((n_narrow, own_rows, LANES), jnp.float32),
            pltpu.SemaphoreType.DMA,
            pltpu.SemaphoreType.DMA((n_wide,)),
            pltpu.SemaphoreType.DMA,
            pltpu.SemaphoreType.DMA((n_narrow,)),
            pltpu.SemaphoreType.DMA((n_narrow,)),
        ],
        compiler_params=pltpu.CompilerParams(
            collective_id=0, has_side_effects=True, vmem_limit_bytes=48 << 20
        ),
    )(amp_tiles, integrals, row_sym, pair_sym)


def solution(mesh):
    in_specs = (P("wide", "narrow"), P("narrow", "wide"), P("wide", None), P(), P(), P())
    out_specs = P(("wide", "narrow"), None)
    return jax.shard_map(
        functools.partial(shards, mesh.shape["wide"], mesh.shape["narrow"]),
        mesh=mesh, in_specs=in_specs, out_specs=out_specs, check_vma=False,
    )
```

time: 241 us -> 56 us (0.23)
  waiting for transfers between devices: 182 us -> 0 us
  Pallas kernels: 0 us -> 49.6 us
  other arithmetic: 36.5 us -> 1.66 us
  between operations: 13.4 us -> 0.03 us
  matrix products: 4.07 us -> 0 us
    all_gather x1 -> x0, waiting for transfers between devices: 142 us -> none  [shards(): gathered = lax.all_gather(amp_tiles, 'wide', axis=1, tiled=True)]
    pallas_call x0 -> x1, Pallas kernels: none -> 49.6 us  [shards(): pl.pallas_call(kernel, out_shape=jax.ShapeDtypeStruct((own_rows, pairs),...]
    reduce_scatter x1 -> x0, waiting for transfers between devices: 39.1 us -> none  [shards(): lax.psum_scatter(jnp.where(keep, block, jnp.zeros_like(block)), 'narrow',...]
    all_gather x1 -> x0, other arithmetic: 34.8 us -> none  [shards(): gathered = lax.all_gather(amp_tiles, 'wide', axis=1, tiled=True)]
    unnamed x0 -> x9, local copies, waits for them, and re-layouts: none -> 4.44 us
    dot_general x1 -> x0, matrix products: 4.07 us -> none  [shards(): block = jnp.dot(integrals, amplitudes, preferred_element_type=jnp.float32)]
    reshape x1 -> x0, local copies, waits for them, and re-layouts: 3.24 us -> none  [shards(): amplitudes = gathered.reshape(column_count, pair_count)]
  transfers between devices with their start and end apart: 2 -> 0, of which waited for: 2 -> 0; matrix products, arithmetic and copies ran while one was open for 1% -> 0% of each run, Pallas kernels for 0% -> 0%
where the time goes in v1:
time: 56 us; the launch traced here: 55.8 us
  Pallas kernels  49.6 us (89%)
  local copies, waits for them, and re-layouts  4.52 us (8%)
  other arithmetic  1.66 us (3%)
    pallas_call x1, Pallas kernels, shards(): pl.pallas_call(kernel, out_shape=jax.ShapeDtypeStruct((own_rows, pairs),...  49.6 us
    unnamed x9, local copies, waits for them, and re-layouts  4.44 us
    reduce_sum x2, other arithmetic, lookup_irrep(): return jnp.sum(jnp.where(hits, table, 0), axis=-1)  1.65 us

profile of v1, /device:TPU:1, one launch (start us, length us, event | category | flops | bytes accessed | tf_op | source)
XLA Modules:
  0.0 55.8 jit_solution(13594500859241057076)
XLA Ops:
  0.0 0.0 copy-start
  0.0 0.7 %copy-done = s32[256,2]{0,1:T(2,128)S(1)} copy-done((s32[256,2]{0,1:T(2,128)S(1)}, s32[256,2]{0,1:T(2,128)}, u32[]{:S(2)}) %copy-start) | copy-done | bytes 2072
  0.7 0.1 constant_dynamic-slice_fusion
  0.8 0.9 %select_reduce_fusion = s32[32,2]{0,1:T(2,128)S(1)} fusion(s32[512]{0:T(512)} %param.9, s32[32,2]{0,1:T(2,128)S(1)} %constant_dynamic-slice_fusion), kind=kLoop, calls=%fused_computation | loop fusion | flops 98240 | bytes 2560 | tf_op jit(solution)/shard_map/reduce_sum | solution.py:182
  1.6 0.1 copy.11
  1.7 0.1 copy.12
  1.8 0.8 %select_reduce_fusion.1 = s32[96,2]{0,1:T(2,128)S(1)} fusion(s32[16]{0:T(128)} %param.11, s32[96,2]{0,1:T(2,128)} %param.10), kind=kLoop, calls=%fused_computation.2 | loop fusion | flops 9024 | bytes 1600 | tf_op jit(solution)/shard_map/reduce_sum | solution.py:182
  2.6 0.0 copy-start.1
  2.6 2.2 %copy-done.1 = bf16[256,8192]{1,0:T(8,128)(2,1)S(1)} copy-done((bf16[256,8192]{1,0:T(8,128)(2,1)S(1)}, bf16[256,8192]{1,0:T(8,128)(2,1)}, u32[]{:S(2)}) %copy-start.1) | copy-done | bytes 4194328
  4.8 0.0 copy-start.2
  4.8 0.8 %copy-done.2 = bf16[1,12288]{1,0:T(2,128)(2,1)S(1)} copy-done((bf16[1,12288]{1,0:T(2,128)(2,1)S(1)}, bf16[1,12288]{1,0:T(2,128)(2,1)}, u32[]{:S(2)}) %copy-start.2) | copy-done | bytes 24600
  5.6 49.6 %shard_map.64 = f32[32,96]{1,0:T(8,128)S(1)} custom-call(bf16[1,12288]{1,0:T(2,128)(2,1)S(1)} %copy-done.2, bf16[256,8192]{1,0:T(8,128)(2,1)S(1)} %copy-done.1, s32[32,1]{1,0:T(8,128)S(1)} %xor.17.row_sym_ref, s32[1,96]{1,0:T(1,128)S(1)} %xor_bitcast_fusion.pair_sym_ref), custom_call_target="tpu_custom_call" | custom-call | tf_op jit(solution)/shard_map/pallas_call | solution.py:196
  55.2 0.6 %copy.14 = f32[32,96]{1,0:T(8,128)} copy(f32[32,96]{1,0:T(8,128)S(1)} %shard_map.64) | data formatting | bytes 24576
  (3 shorter events, 0.0 us)
Async XLA Ops:
  0.0 0.7 %copy-start = (s32[256,2]{0,1:T(2,128)S(1)}, s32[256,2]{0,1:T(2,128)}, u32[]{:S(2)}) copy-start(s32[256,2]{0,1:T(2,128)} %param.8) | copy-start | bytes 6148
  2.6 2.2 %copy-start.1 = (bf16[256,8192]{1,0:T(8,128)(2,1)S(1)}, bf16[256,8192]{1,0:T(8,128)(2,1)}, u32[]{:S(2)}) copy-start(bf16[256,8192]{1,0:T(8,128)(2,1)} %integrals_ref.1) | copy-start | bytes 12582916
  4.8 0.8 %copy-start.2 = (bf16[1,12288]{1,0:T(2,128)(2,1)S(1)}, bf16[1,12288]{1,0:T(2,128)(2,1)}, u32[]{:S(2)}) copy-start(bf16[1,12288]{1,0:T(2,128)(2,1)} %amp_ref.1) | copy-start | bytes 73732

commit v2 on v1

v2 whole, which is shorter than its diff:
```python
import functools

import jax
import jax.numpy as jnp
from jax import lax
from jax.experimental import pallas as pl
from jax.experimental.pallas import tpu as pltpu
from jax.sharding import PartitionSpec as P

MESH = pl.DeviceIdType.MESH
NX = 4
LANES = 128


def pair_symmetry(orbitals, table):
    count, entries = orbitals.shape[1], table.shape[1]
    diagonal = lax.broadcasted_iota(jnp.int32, (entries, entries), 0) == lax.broadcasted_iota(
        jnp.int32, (entries, entries), 1
    )
    column = jnp.sum(jnp.where(diagonal, table, 0), axis=1, keepdims=True)
    place = lax.broadcasted_iota(jnp.int32, (entries, count), 0)
    first, second = (
        jnp.sum(jnp.where(place == orbitals[i : i + 1, :], column, 0), axis=0, keepdims=True) for i in range(2)
    )
    return first ^ second


def kernel(
    integrals_ref, amp_ref, row_orbitals_ref, orb_ref, pairs_ref, occ_ref, out_ref,
    tile, row_orbitals, orb, occ_pairs, occ, row_sym, rows, upright, gathered, block, acc, parts,
    load_sem, small_sem, arrive, sent, part_sent, part_arrive,
):
    n_wide, n_narrow = lax.axis_size("wide"), lax.axis_size("narrow")
    nz = n_wide // NX
    half = nz // 2
    pairs = gathered.shape[1]
    own_rows = out_ref.shape[0]
    wide, narrow = lax.axis_index("wide"), lax.axis_index("narrow")
    z, x = wide // NX, wide % NX

    def at(dz, dx):
        return ((z + dz + nz) % nz) * NX + (x + dx + NX) % NX

    targets = [(sign * d, dx) for dx in (0, 1) for d in (1, 2) for sign in (1, -1)] + [(0, 1), (0, -1)]
    barrier = pltpu.get_barrier_semaphore()
    for dz, dx in targets:
        pl.semaphore_signal(barrier, inc=1, device_id={"wide": at(-dz, -dx)}, device_id_type=MESH)
    for step in range(1, n_narrow):
        pl.semaphore_signal(
            barrier, inc=1, device_id={"narrow": (narrow + step) % n_narrow}, device_id_type=MESH
        )

    small = [
        pltpu.make_async_copy(source, target, small_sem.at[i])
        for i, (source, target) in enumerate(
            (
                (amp_ref, tile), (row_orbitals_ref, row_orbitals), (orb_ref, orb), (pairs_ref, occ_pairs),
                (occ_ref, occ),
            )
        )
    ]
    for copy in small:
        copy.start()
    load = pltpu.make_async_copy(integrals_ref, block, load_sem)
    load.start()

    upright[...] = jnp.zeros_like(upright)
    acc[...] = jnp.zeros_like(acc)
    small[0].wait()
    period = 4 * pairs
    groups = tile.shape[1] // period
    for g in range(groups):
        rows[g : g + 1, :] = tile[0:1, g * period : (g + 1) * period].astype(jnp.float32)
    for j in range(4):
        upright[pl.ds(j, groups, stride=4), 0:pairs] = rows[:, j * pairs : (j + 1) * pairs]
    gathered[wide] = upright[...].T[:pairs, :].astype(jnp.bfloat16)

    pl.semaphore_wait(barrier, len(targets) + n_narrow - 1)

    def copy_of(source, dz, dx):
        return pltpu.make_async_remote_copy(
            src_ref=gathered.at[source],
            dst_ref=gathered.at[source],
            send_sem=sent,
            recv_sem=arrive.at[source],
            device_id={"wide": at(dz, dx)},
            device_id_type=MESH,
        )

    def send(source, dz, dx):
        copy_of(source, dz, dx).start()

    def wait(source):
        copy_of(source, 1, 0).wait_recv()

    def multiply(dz):
        wait(at(dz, 1))
        wait(at(dz, -2))
        base = ((z + dz + nz) % nz) * NX
        columns = pl.ds(pl.multiple_of(base * LANES, NX * LANES), NX * LANES)
        amplitudes = jnp.concatenate([gathered[base + i] for i in range(NX)], axis=1)
        acc[:, 0:pairs] += lax.dot_general(
            block[:, columns], amplitudes, (((1,), (1,)), ((), ())), preferred_element_type=jnp.float32
        )

    last = half // 2 - 1
    forward = ((1, 0, True), (-1, 1, True), (-1, 0, False), (1, 1, False))
    for sign, dx, far in forward:
        if far or last > 0:
            send(wide, 2 * sign, dx)
    for sign, dx, _ in forward:
        send(wide, sign, dx)
    send(wide, 0, 1)
    send(wide, 0, -1)

    for copy in small[1:]:
        copy.wait()
    symmetry = pair_symmetry(row_orbitals[...], orb[...])
    n_rows = symmetry.shape[1]
    diagonal = lax.broadcasted_iota(jnp.int32, (n_rows, n_rows), 0) == lax.broadcasted_iota(
        jnp.int32, (n_rows, n_rows), 1
    )
    row_sym[...] = jnp.broadcast_to(
        jnp.sum(jnp.where(diagonal, symmetry, 0), axis=1, keepdims=True), row_sym.shape
    )
    own_sym = row_sym[pl.ds(pl.multiple_of(narrow * own_rows, own_rows), own_rows), 0:pairs]
    keep = own_sym == pair_symmetry(occ_pairs[...], occ[...])

    beside = at(0, -1)
    wait(beside)
    send(beside, 0, 1)
    load.wait()

    for k in range(1, last + 1):
        for sign, dx, far in forward:
            source = at(-2 * k * sign, -dx)
            wait(source)
            if far or k < last:
                send(source, 2 * sign, 0)
            send(source, sign, 0)
            send(source, 0, 1 if dx else -1)
        for sign, dx, _ in forward:
            source = at(-(2 * k - 1) * sign, -dx)
            wait(source)
            send(source, 0, 1 if dx else -1)
        if k == 1:
            multiply(0)
        else:
            for d in (2 * k - 3, 2 * k - 2):
                multiply(d)
                multiply(-d)
    for sign, dx, far in forward:
        if far:
            source = at(-half * sign, -dx)
            wait(source)
            send(source, 0, 1 if dx else -1)
        source = at(-(half - 1) * sign, -dx)
        wait(source)
        send(source, 0, 1 if dx else -1)
    for d in range(max(half - 3, 1), half):
        multiply(d)
        multiply(-d)
    multiply(half)

    def part(step):
        to = (narrow + step) % n_narrow
        return pltpu.make_async_remote_copy(
            src_ref=acc.at[pl.ds(pl.multiple_of(to * own_rows, own_rows), own_rows)],
            dst_ref=parts.at[n_narrow - step],
            send_sem=part_sent.at[step],
            recv_sem=part_arrive.at[n_narrow - step],
            device_id={"narrow": to},
            device_id_type=MESH,
        )

    copies = [part(step) for step in range(1, n_narrow)]
    for copy in copies:
        copy.start()
    total = acc[pl.ds(pl.multiple_of(narrow * own_rows, own_rows), own_rows), :]
    for step, copy in zip(range(1, n_narrow), copies):
        pltpu.make_async_remote_copy(
            src_ref=parts.at[step],
            dst_ref=parts.at[step],
            send_sem=part_sent.at[step],
            recv_sem=part_arrive.at[step],
            device_id={"narrow": (narrow + step) % n_narrow},
            device_id_type=MESH,
        ).wait_recv()
        total += parts[step]
    out_ref[...] = jnp.where(keep, total[:, 0:pairs], 0.0)
    for copy in copies:
        copy.wait_send()
    pltpu.make_async_remote_copy(
        src_ref=gathered.at[pl.ds(0, n_wide - 1)],
        dst_ref=gathered.at[pl.ds(0, n_wide - 1)],
        send_sem=sent,
        recv_sem=arrive.at[0],
        device_id={"wide": at(1, 0)},
        device_id_type=MESH,
    ).wait_send()


def shards(n_wide, n_narrow, integrals, amp_tiles, row_orbitals, orb_irrep, occ_pairs, occ_irrep):
    pairs = occ_pairs.shape[0]
    n_rows, n_columns = integrals.shape
    own_rows = n_rows // n_narrow
    operands = (
        integrals, amp_tiles, row_orbitals.T, orb_irrep[None, :], occ_pairs.T, occ_irrep[None, :],
    )
    return pl.pallas_call(
        kernel,
        out_shape=jax.ShapeDtypeStruct((own_rows, pairs), jnp.float32),
        in_specs=[pl.BlockSpec(memory_space=pltpu.HBM)] * len(operands),
        out_specs=pl.BlockSpec(memory_space=pltpu.VMEM),
        scratch_shapes=[
            *(pltpu.VMEM(a.shape, a.dtype) for a in operands[1:]),
            pltpu.VMEM((n_rows, LANES), jnp.int32),
            pltpu.VMEM((LANES // 4, 4 * pairs), jnp.float32),
            pltpu.VMEM((LANES, LANES), jnp.float32),
            pltpu.VMEM((n_wide, pairs, LANES), jnp.bfloat16),
            pltpu.VMEM((n_rows, n_columns), jnp.bfloat16),
            pltpu.VMEM((n_rows, LANES), jnp.float32),
            pltpu.VMEM((n_narrow, own_rows, LANES), jnp.float32),
            pltpu.SemaphoreType.DMA,
            pltpu.SemaphoreType.DMA((len(operands) - 1,)),
            pltpu.SemaphoreType.DMA((n_wide,)),
            pltpu.SemaphoreType.DMA,
            pltpu.SemaphoreType.DMA((n_narrow,)),
            pltpu.SemaphoreType.DMA((n_narrow,)),
        ],
        compiler_params=pltpu.CompilerParams(
            collective_id=0, has_side_effects=True, vmem_limit_bytes=32 << 20
        ),
    )(*operands)


def solution(mesh):
    in_specs = (P("wide", "narrow"), P("narrow", "wide"), P("wide", None), P(), P(), P())
    out_specs = P(("wide", "narrow"), None)
    return jax.shard_map(
        functools.partial(shards, mesh.shape["wide"], mesh.shape["narrow"]),
        mesh=mesh, in_specs=in_specs, out_specs=out_specs, check_vma=False,
    )
```

time: 56 us -> 46.8 us (0.84)
  Pallas kernels: 49.6 us -> 40.2 us
  local copies, waits for them, and re-layouts: 4.52 us -> 6.29 us
  other arithmetic: 1.66 us -> 0 us
    pallas_call x1, Pallas kernels: 49.6 us -> 40.2 us  [shards(): pl.pallas_call(kernel, out_shape=jax.ShapeDtypeStruct((own_rows, pairs),...]
    unnamed x9 -> x13, local copies, waits for them, and re-layouts: 4.44 us -> 6.29 us
    reduce_sum x2 -> x0, other arithmetic: 1.65 us -> none  [lookup_irrep(): return jnp.sum(jnp.where(hits, table, 0), axis=-1)]
where the time goes in v2:
time: 46.8 us; the launch traced here: 46.5 us
  Pallas kernels  40.2 us (86%)
  local copies, waits for them, and re-layouts  6.29 us (13%)
    pallas_call x1, Pallas kernels, shards(): pl.pallas_call(kernel, out_shape=jax.ShapeDtypeStruct((own_rows, pairs),...  40.2 us
    unnamed x13, local copies, waits for them, and re-layouts  6.29 us

profile of v2, /device:TPU:1, one launch (start us, length us, event | category | flops | bytes accessed | tf_op | source)
XLA Modules:
  0.0 46.5 jit_solution(732006767823656018)
XLA Ops:
  0.0 0.0 copy-start
  0.0 2.2 %copy-done = bf16[256,8192]{1,0:T(8,128)(2,1)S(1)} copy-done((bf16[256,8192]{1,0:T(8,128)(2,1)S(1)}, bf16[256,8192]{1,0:T(8,128)(2,1)}, u32[]{:S(2)}) %copy-start) | copy-done | bytes 4194328
  2.2 0.0 copy-start.1
  2.2 0.8 %copy-done.1 = bf16[1,12288]{1,0:T(2,128)(2,1)S(1)} copy-done((bf16[1,12288]{1,0:T(2,128)(2,1)S(1)}, bf16[1,12288]{1,0:T(2,128)(2,1)}, u32[]{:S(2)}) %copy-start.1) | copy-done | bytes 24600
  3.0 0.0 copy-start.2
  3.0 0.7 %copy-done.2 = s32[256,2]{0,1:T(2,128)S(1)} copy-done((s32[256,2]{0,1:T(2,128)S(1)}, s32[256,2]{0,1:T(2,128)}, u32[]{:S(2)}) %copy-start.2) | copy-done | bytes 2072
  3.7 0.0 copy-start.3
  3.7 0.7 %copy-done.3 = s32[512]{0:T(512)S(1)} copy-done((s32[512]{0:T(512)S(1)}, s32[512]{0:T(512)}, u32[]{:S(2)}) %copy-start.3) | copy-done | bytes 2072
  4.4 0.0 copy-start.4
  4.4 0.7 %copy-done.4 = s32[96,2]{0,1:T(2,128)S(1)} copy-done((s32[96,2]{0,1:T(2,128)S(1)}, s32[96,2]{0,1:T(2,128)}, u32[]{:S(2)}) %copy-start.4) | copy-done | bytes 792
  5.0 0.0 copy-start.5
  5.0 0.7 %copy-done.5 = s32[16]{0:T(128)S(1)} copy-done((s32[16]{0:T(128)S(1)}, s32[16]{0:T(128)}, u32[]{:S(2)}) %copy-start.5) | copy-done | bytes 88
  5.7 40.2 %shard_map.64 = f32[32,96]{1,0:T(8,128)S(1)} custom-call(bf16[256,8192]{1,0:T(8,128)(2,1)S(1)} %copy-done, bf16[1,12288]{1,0:T(2,128)(2,1)S(1)} %copy-done.1, s32[2,256]{1,0:T(2,128)S(1)} %bitcast.4, s32[1,512]{1,0:T(1,128)S(1)} %bitcast.5, s32[2,96]{1,0:T(2,128)S(1)} %bitcast.6, s32[1,16]{1,0:T(1,128)S(1)} %bitcast.7), custom_call_target="tpu_custom_call" | custom-call | tf_op jit(solution)/shard_map/pallas_call | solution.py:210
  45.9 0.6 %copy.8 = f32[32,96]{1,0:T(8,128)} copy(f32[32,96]{1,0:T(8,128)S(1)} %shard_map.64) | data formatting | bytes 24576
Async XLA Ops:
  0.0 2.2 %copy-start = (bf16[256,8192]{1,0:T(8,128)(2,1)S(1)}, bf16[256,8192]{1,0:T(8,128)(2,1)}, u32[]{:S(2)}) copy-start(bf16[256,8192]{1,0:T(8,128)(2,1)} %integrals_ref.1) | copy-start | bytes 12582916
  2.2 0.8 %copy-start.1 = (bf16[1,12288]{1,0:T(2,128)(2,1)S(1)}, bf16[1,12288]{1,0:T(2,128)(2,1)}, u32[]{:S(2)}) copy-start(bf16[1,12288]{1,0:T(2,128)(2,1)} %amp_ref.1) | copy-start | bytes 73732
  3.0 0.7 %copy-start.2 = (s32[256,2]{0,1:T(2,128)S(1)}, s32[256,2]{0,1:T(2,128)}, u32[]{:S(2)}) copy-start(s32[256,2]{0,1:T(2,128)} %param.8) | copy-start | bytes 6148
  3.7 0.7 %copy-start.3 = (s32[512]{0:T(512)S(1)}, s32[512]{0:T(512)}, u32[]{:S(2)}) copy-start(s32[512]{0:T(512)} %param.9) | copy-start | bytes 6148
  4.4 0.7 %copy-start.4 = (s32[96,2]{0,1:T(2,128)S(1)}, s32[96,2]{0,1:T(2,128)}, u32[]{:S(2)}) copy-start(s32[96,2]{0,1:T(2,128)} %param.10) | copy-start | bytes 2308
  5.0 0.7 %copy-start.5 = (s32[16]{0:T(128)S(1)}, s32[16]{0:T(128)}, u32[]{:S(2)}) copy-start(s32[16]{0:T(128)} %param.11) | copy-start | bytes 196
